TPU v7x, 32 devices: a whole 2x2x4 slice. The times are simulated.
32 devices in a mesh: people: 8 (over z, x), snps: 4 (over y, core).
Axes of the slice: x: 2, y: 2, z: 4, core: 2. Of those that a mesh axis runs over, the one named last changes fastest.
Arguments:
- genotype: bfloat16 [4096, 16384], P('people', 'snps'), may hold values from 0 to 2, as said below
- residual_init: float32 [32, 4096], P(None, 'people'), may hold values from -30 to 30
- effects_init: float32 [32, 16384], P(None, 'snps'), may hold values from -3 to 3
- allele_freq: float32 [16384], P('snps'), may hold values from 0.05 to 0.5, as said below
- snp_scale: float32 [16384], P('snps'), may hold values from 0.8 to 1.25
- ld_basis: bfloat16 [32, 512, 512], P('snps'), may hold values from -1 to 1, as said below
- ld_eig: float32 [16384], P('snps'), may hold values from 0.5 to 2
- ridge: float32 [32], replicated, may hold values from 1.5 to 4
- noise_scale: float32 [32], replicated, may hold values from 0.2 to 1
- normal_draws: bfloat16 [4, 32, 16384], P(None, None, 'snps'), may hold values from -5 to 5
- assignment: int32 [32], P('snps'), may hold values from 0 to 7, as said below
Outputs:
- effects: float32 [32, 16384], P(None, 'snps')
- residual: float32 [32, 4096], P(None, 'people')
Inputs may be any that keep to these rules, and one draw needn't show every extreme that they name: `assignment`: the 8 entries that lie on one index of snps are each a permutation of 0 to 7. `ld_basis`: each block's basis is orthogonal up to its rounding to bfloat16. `genotype`: only the values 0, 1 and 2 occur; each dosage counts two alleles, each present with the SNP's allele_freq. `allele_freq`: multiples of 0.001.
All inputs are finite; a program needn't handle non-finite values.
Results may differ from a plain program's by a relative error of at most 0.014.
Values sent between devices are 32-bit elements; how exact they have to be, the bound alone decides.
A program may use at most 64 MiB of HBM per device.

v0:
```python
import jax
import jax.numpy as jnp
from jax import lax
from jax.sharding import PartitionSpec as P

WINDOW = 4
GROUPS_DEV = 2


def contract_last(left, right):
    return lax.dot_general(
        left, right, (((1,), (1,)), ((), ())), preferred_element_type=jnp.float32
    )


def sum_block(stacked):
    return lax.psum(stacked, "people")


def sample_block(summed_row, old_effects, block_basis, block_eig, draws_block, spread, ridge):
    prior = jnp.dot(
        old_effects.astype(jnp.bfloat16), block_basis, preferred_element_type=jnp.float32
    )
    coupled = contract_last((prior * block_eig[None, :]).astype(jnp.bfloat16), block_basis)
    rotated = jnp.dot(
        (summed_row + coupled).astype(jnp.bfloat16), block_basis, preferred_element_type=jnp.float32
    )
    precision = block_eig[None, :] + ridge[:, None]
    sampled = rotated / precision + spread[:, None] * draws_block.astype(jnp.float32) / jnp.sqrt(
        precision
    )
    return contract_last(sampled.astype(jnp.bfloat16), block_basis)


def per_device(
    genotype,
    residual_init,
    effects_init,
    allele_freq,
    snp_scale,
    ld_basis,
    ld_eig,
    ridge,
    noise_scale,
    normal_draws,
    assignment,
):
    block_width = ld_basis.shape[1]
    people_total = genotype.shape[0] * lax.axis_size("people")
    col_scale = snp_scale / jnp.sqrt(people_total * 2.0 * allele_freq * (1.0 - allele_freq))
    residual = residual_init
    effects = effects_init
    for round_idx in range(normal_draws.shape[0]):
        start_residual = residual
        local_squares = jnp.sum(residual * residual, axis=1)
        spread = None
        sum_squares = lax.psum(local_squares, "people")
        spread = noise_scale * jnp.sqrt(sum_squares / people_total + 1e-06)
        states = [residual for member in range(GROUPS_DEV)]
        plan = [[(member, slot_idx)] for member in range(GROUPS_DEV) for slot_idx in range(WINDOW)]
        for step_index, members in enumerate(plan):
            prepared = []
            partials = []
            for member, slot_idx in members:
                local_block = assignment[member * WINDOW + slot_idx]
                col_start = local_block * block_width
                block_x = lax.dynamic_slice_in_dim(genotype, col_start, block_width, 1)
                block_freq = lax.dynamic_slice_in_dim(allele_freq, col_start, block_width, 0)
                block_scale = lax.dynamic_slice_in_dim(col_scale, col_start, block_width, 0)
                state = states[member]
                cross_term = jnp.dot(
                    state.astype(jnp.bfloat16), block_x, preferred_element_type=jnp.float32
                )
                partial_value = block_scale[None, :] * (
                    cross_term - 2.0 * block_freq[None, :] * jnp.sum(state, axis=1)[:, None]
                )
                partials.append(partial_value)
                prepared.append((member, local_block, col_start, block_x, block_freq, block_scale))
            stacked = jnp.stack(partials, axis=0)
            summed = sum_block(stacked)
            for position, entry in enumerate(prepared):
                member, local_block, col_start, block_x, block_freq, block_scale = entry
                block_basis = lax.dynamic_index_in_dim(ld_basis, local_block, 0, keepdims=False)
                block_eig = lax.dynamic_slice_in_dim(ld_eig, col_start, block_width, 0)
                old_effects = lax.dynamic_slice_in_dim(effects, col_start, block_width, 1)
                draws_block = lax.dynamic_slice_in_dim(
                    normal_draws[round_idx], col_start, block_width, 1
                )
                fresh = sample_block(
                    summed[position],
                    old_effects,
                    block_basis,
                    block_eig,
                    draws_block,
                    spread,
                    ridge,
                )
                change = fresh - old_effects
                effects = lax.dynamic_update_slice_in_dim(effects, fresh, col_start, 1)
                weighted = change * block_scale[None, :]
                shift_term = 2.0 * jnp.sum(weighted * block_freq[None, :], axis=1)
                states[member] = (
                    states[member]
                    - contract_last(weighted.astype(jnp.bfloat16), block_x)
                    + shift_term[:, None]
                )
        local_changes = states[0] - start_residual
        member = 1
        local_changes = local_changes + (states[member] - start_residual)
        residual = start_residual + lax.psum(local_changes, "snps")
    return (effects, residual)


def solution(mesh):
    return jax.shard_map(
        per_device,
        mesh=mesh,
        in_specs=(
            P("people", "snps"),
            P(None, "people"),
            P(None, "snps"),
            P("snps"),
            P("snps"),
            P("snps", None, None),
            P("snps"),
            P(),
            P(),
            P(None, None, "snps"),
            P("snps"),
        ),
        out_specs=(P(None, "snps"), P(None, "people")),
        check_vma=False,
    )
```

profile of v0, /device:TPU:0, one launch (start us, length us, event | category | flops | bytes accessed | tf_op | source)
XLA Modules:
  0.0 2370.5 jit_solution(16344473810487242396)
XLA Ops:
  62.1 28.9 %all-reduce.37.cloned.1.call-done = f32[32,512]{1,0:T(8,128)} async-done(((f32[32,512]{1,0:T(8,128)}), f32[32,512]{1,0:T(8,128)}) %all-reduce.37.cloned.1.call-update) | async-done | bytes 65552 | tf_op jit(solution)/shard_map/psum | solution.py:17
  98.8 68.2 %all-reduce.39.cloned.1.call-done = f32[32,512]{1,0:T(8,128)} async-done(((f32[32,512]{1,0:T(8,128)}), f32[32,512]{1,0:T(8,128)}) %all-reduce.39.cloned.1.call-update) | async-done | bytes 65552 | tf_op jit(solution)/shard_map/psum | solution.py:17
  174.8 68.0 %all-reduce.41.cloned.1.call-done = f32[32,512]{1,0:T(8,128)} async-done(((f32[32,512]{1,0:T(8,128)}), f32[32,512]{1,0:T(8,128)}) %all-reduce.41.cloned.1.call-update) | async-done | bytes 65552 | tf_op jit(solution)/shard_map/psum | solution.py:17
  250.5 69.5 %all-reduce.99.cloned.1.call-done = (f32[32,512]{1,0:T(8,128)}, f32[32,512]{1,0:T(8,128)}) async-done(((f32[32,512]{1,0:T(8,128)}, f32[32,512]{1,0:T(8,128)}), (f32[32,512]{1,0:T(8,128)}, f32[32,512]{1,0:T(8,128)})) %all-reduce.99.cloned.1.call-update) | async-done | bytes 131088 | tf_op jit(solution)/shard_map/psum | solution.py:17
  332.8 66.7 %all-reduce.43.cloned.1.call-done = f32[32,512]{1,0:T(8,128)} async-done(((f32[32,512]{1,0:T(8,128)}), f32[32,512]{1,0:T(8,128)}) %all-reduce.43.cloned.1.call-update) | async-done | bytes 65552 | tf_op jit(solution)/shard_map/psum | solution.py:17
  407.3 68.0 %all-reduce.45.cloned.1.call-done = f32[32,512]{1,0:T(8,128)} async-done(((f32[32,512]{1,0:T(8,128)}), f32[32,512]{1,0:T(8,128)}) %all-reduce.45.cloned.1.call-update) | async-done | bytes 65552 | tf_op jit(solution)/shard_map/psum | solution.py:17
  483.2 67.9 %all-reduce.47.cloned.1.call-done = f32[32,512]{1,0:T(8,128)} async-done(((f32[32,512]{1,0:T(8,128)}), f32[32,512]{1,0:T(8,128)}) %all-reduce.47.cloned.1.call-update) | async-done | bytes 65552 | tf_op jit(solution)/shard_map/psum | solution.py:17
  558.9 30.3 %all-reduce.49.cloned.1.call-done = f32[32,512]{1,0:T(8,128)} async-done(((f32[32,512]{1,0:T(8,128)}), f32[32,512]{1,0:T(8,128)}) %all-reduce.49.cloned.1.call-update) | async-done | bytes 65552 | tf_op jit(solution)/shard_map/psum | solution.py:110
  615.3 65.6 %all-reduce.51.cloned.1.call-done = f32[32,512]{1,0:T(8,128)} async-done(((f32[32,512]{1,0:T(8,128)}), f32[32,512]{1,0:T(8,128)}) %all-reduce.51.cloned.1.call-update) | async-done | bytes 65552 | tf_op jit(solution)/shard_map/psum | solution.py:17
  688.7 68.1 %all-reduce.53.cloned.1.call-done = f32[32,512]{1,0:T(8,128)} async-done(((f32[32,512]{1,0:T(8,128)}), f32[32,512]{1,0:T(8,128)}) %all-reduce.53.cloned.1.call-update) | async-done | bytes 65552 | tf_op jit(solution)/shard_map/psum | solution.py:17
  764.6 68.0 %all-reduce.55.cloned.1.call-done = f32[32,512]{1,0:T(8,128)} async-done(((f32[32,512]{1,0:T(8,128)}), f32[32,512]{1,0:T(8,128)}) %all-reduce.55.cloned.1.call-update) | async-done | bytes 65552 | tf_op jit(solution)/shard_map/psum | solution.py:17
  840.5 69.5 %all-reduce.97.cloned.1.call-done = (f32[32,512]{1,0:T(8,128)}, f32[32,512]{1,0:T(8,128)}) async-done(((f32[32,512]{1,0:T(8,128)}, f32[32,512]{1,0:T(8,128)}), (f32[32,512]{1,0:T(8,128)}, f32[32,512]{1,0:T(8,128)})) %all-reduce.97.cloned.1.call-update) | async-done | bytes 131088 | tf_op jit(solution)/shard_map/psum | solution.py:17
  922.3 68.4 %all-reduce.57.cloned.1.call-done = f32[32,512]{1,0:T(8,128)} async-done(((f32[32,512]{1,0:T(8,128)}), f32[32,512]{1,0:T(8,128)}) %all-reduce.57.cloned.1.call-update) | async-done | bytes 65552 | tf_op jit(solution)/shard_map/psum | solution.py:17
  998.7 67.8 %all-reduce.59.cloned.1.call-done = f32[32,512]{1,0:T(8,128)} async-done(((f32[32,512]{1,0:T(8,128)}), f32[32,512]{1,0:T(8,128)}) %all-reduce.59.cloned.1.call-update) | async-done | bytes 65552 | tf_op jit(solution)/shard_map/psum | solution.py:17
  1074.5 67.8 %all-reduce.61.cloned.1.call-done = f32[32,512]{1,0:T(8,128)} async-done(((f32[32,512]{1,0:T(8,128)}), f32[32,512]{1,0:T(8,128)}) %all-reduce.61.cloned.1.call-update) | async-done | bytes 65552 | tf_op jit(solution)/shard_map/psum | solution.py:17
  1150.1 30.3 %all-reduce.63.cloned.1.call-done = f32[32,512]{1,0:T(8,128)} async-done(((f32[32,512]{1,0:T(8,128)}), f32[32,512]{1,0:T(8,128)}) %all-reduce.63.cloned.1.call-update) | async-done | bytes 65552 | tf_op jit(solution)/shard_map/psum | solution.py:110
  1206.5 65.6 %all-reduce.65.cloned.1.call-done = f32[32,512]{1,0:T(8,128)} async-done(((f32[32,512]{1,0:T(8,128)}), f32[32,512]{1,0:T(8,128)}) %all-reduce.65.cloned.1.call-update) | async-done | bytes 65552 | tf_op jit(solution)/shard_map/psum | solution.py:17
  1279.9 68.1 %all-reduce.67.cloned.1.call-done = f32[32,512]{1,0:T(8,128)} async-done(((f32[32,512]{1,0:T(8,128)}), f32[32,512]{1,0:T(8,128)}) %all-reduce.67.cloned.1.call-update) | async-done | bytes 65552 | tf_op jit(solution)/shard_map/psum | solution.py:17
  1355.8 68.0 %all-reduce.69.cloned.1.call-done = f32[32,512]{1,0:T(8,128)} async-done(((f32[32,512]{1,0:T(8,128)}), f32[32,512]{1,0:T(8,128)}) %all-reduce.69.cloned.1.call-update) | async-done | bytes 65552 | tf_op jit(solution)/shard_map/psum | solution.py:17
  1431.6 69.5 %all-reduce.95.cloned.1.call-done = (f32[32,512]{1,0:T(8,128)}, f32[32,512]{1,0:T(8,128)}) async-done(((f32[32,512]{1,0:T(8,128)}, f32[32,512]{1,0:T(8,128)}), (f32[32,512]{1,0:T(8,128)}, f32[32,512]{1,0:T(8,128)})) %all-reduce.95.cloned.1.call-update) | async-done | bytes 131088 | tf_op jit(solution)/shard_map/psum | solution.py:17
  1513.3 68.4 %all-reduce.71.cloned.1.call-done = f32[32,512]{1,0:T(8,128)} async-done(((f32[32,512]{1,0:T(8,128)}), f32[32,512]{1,0:T(8,128)}) %all-reduce.71.cloned.1.call-update) | async-done | bytes 65552 | tf_op jit(solution)/shard_map/psum | solution.py:17
  1589.5 68.0 %all-reduce.73.cloned.1.call-done = f32[32,512]{1,0:T(8,128)} async-done(((f32[32,512]{1,0:T(8,128)}), f32[32,512]{1,0:T(8,128)}) %all-reduce.73.cloned.1.call-update) | async-done | bytes 65552 | tf_op jit(solution)/shard_map/psum | solution.py:17
  1665.4 67.9 %all-reduce.75.cloned.1.call-done = f32[32,512]{1,0:T(8,128)} async-done(((f32[32,512]{1,0:T(8,128)}), f32[32,512]{1,0:T(8,128)}) %all-reduce.75.cloned.1.call-update) | async-done | bytes 65552 | tf_op jit(solution)/shard_map/psum | solution.py:17
  1741.0 30.3 %all-reduce.77.cloned.1.call-done = f32[32,512]{1,0:T(8,128)} async-done(((f32[32,512]{1,0:T(8,128)}), f32[32,512]{1,0:T(8,128)}) %all-reduce.77.cloned.1.call-update) | async-done | bytes 65552 | tf_op jit(solution)/shard_map/psum | solution.py:110
  1797.4 65.6 %all-reduce.79.cloned.1.call-done = f32[32,512]{1,0:T(8,128)} async-done(((f32[32,512]{1,0:T(8,128)}), f32[32,512]{1,0:T(8,128)}) %all-reduce.79.cloned.1.call-update) | async-done | bytes 65552 | tf_op jit(solution)/shard_map/psum | solution.py:17
  1870.8 68.2 %all-reduce.81.cloned.1.call-done = f32[32,512]{1,0:T(8,128)} async-done(((f32[32,512]{1,0:T(8,128)}), f32[32,512]{1,0:T(8,128)}) %all-reduce.81.cloned.1.call-update) | async-done | bytes 65552 | tf_op jit(solution)/shard_map/psum | solution.py:17
  1946.7 68.0 %all-reduce.83.cloned.1.call-done = f32[32,512]{1,0:T(8,128)} async-done(((f32[32,512]{1,0:T(8,128)}), f32[32,512]{1,0:T(8,128)}) %all-reduce.83.cloned.1.call-update) | async-done | bytes 65552 | tf_op jit(solution)/shard_map/psum | solution.py:17
  2022.5 69.5 %all-reduce.93.cloned.1.call-done = (f32[32,512]{1,0:T(8,128)}, f32[32,512]{1,0:T(8,128)}) async-done(((f32[32,512]{1,0:T(8,128)}, f32[32,512]{1,0:T(8,128)}), (f32[32,512]{1,0:T(8,128)}, f32[32,512]{1,0:T(8,128)})) %all-reduce.93.cloned.1.call-update) | async-done | bytes 131088 | tf_op jit(solution)/shard_map/psum | solution.py:17
  2104.2 68.4 %all-reduce.85.cloned.1.call-done = f32[32,512]{1,0:T(8,128)} async-done(((f32[32,512]{1,0:T(8,128)}), f32[32,512]{1,0:T(8,128)}) %all-reduce.85.cloned.1.call-update) | async-done | bytes 65552 | tf_op jit(solution)/shard_map/psum | solution.py:17
  2180.4 68.0 %all-reduce.87.cloned.1.call-done = f32[32,512]{1,0:T(8,128)} async-done(((f32[32,512]{1,0:T(8,128)}), f32[32,512]{1,0:T(8,128)}) %all-reduce.87.cloned.1.call-update) | async-done | bytes 65552 | tf_op jit(solution)/shard_map/psum | solution.py:17
  2256.3 67.9 %all-reduce.89.cloned.1.call-done = f32[32,512]{1,0:T(8,128)} async-done(((f32[32,512]{1,0:T(8,128)}), f32[32,512]{1,0:T(8,128)}) %all-reduce.89.cloned.1.call-update) | async-done | bytes 65552 | tf_op jit(solution)/shard_map/psum | solution.py:17
  2330.8 31.6 %all-reduce.91.cloned.1.call-done = f32[32,512]{1,0:T(8,128)} async-done(((f32[32,512]{1,0:T(8,128)}), f32[32,512]{1,0:T(8,128)}) %all-reduce.91.cloned.1.call-update) | async-done | bytes 65552 | tf_op jit(solution)/shard_map/psum | solution.py:110
  (380 shorter events, 349.0 us)
Async XLA Ops:
  7.2 83.7 %all-reduce.37.cloned.1.call-start = ((), (), s32[]{:S(2)}) async-start(), calls=%async_computation | async-start | bytes 131072 | tf_op jit(solution)/shard_map/psum | solution.py:17
  18.7 148.3 %all-reduce.39.cloned.1.call-start = ((), (), s32[]{:S(2)}) async-start(), calls=%async_computation.1 | async-start | bytes 131072 | tf_op jit(solution)/shard_map/psum | solution.py:17
  97.5 145.3 %all-reduce.41.cloned.1.call-start = ((), (), s32[]{:S(2)}) async-start(), calls=%async_computation.2 | async-start | bytes 131072 | tf_op jit(solution)/shard_map/psum | solution.py:17
  173.4 146.7 %all-reduce.99.cloned.1.call-start = ((), (), s32[]{:S(2)}) async-start(), calls=%async_computation.31 | async-start | bytes 262144 | tf_op jit(solution)/shard_map/psum | solution.py:17
  249.2 150.2 %all-reduce.43.cloned.1.call-start = ((), (), s32[]{:S(2)}) async-start(), calls=%async_computation.3 | async-start | bytes 131072 | tf_op jit(solution)/shard_map/psum | solution.py:17
  330.9 144.3 %all-reduce.45.cloned.1.call-start = ((), (), s32[]{:S(2)}) async-start(), calls=%async_computation.4 | async-start | bytes 131072 | tf_op jit(solution)/shard_map/psum | solution.py:17
  406.0 145.1 %all-reduce.47.cloned.1.call-start = ((), (), s32[]{:S(2)}) async-start(), calls=%async_computation.5 | async-start | bytes 131072 | tf_op jit(solution)/shard_map/psum | solution.py:17
  481.9 107.3 %all-reduce.49.cloned.1.call-start = ((), (), s32[]{:S(2)}) async-start(), calls=%async_computation.6 | async-start | bytes 131072 | tf_op jit(solution)/shard_map/psum | solution.py:110
  557.5 123.4 %all-reduce.51.cloned.1.call-start = ((), (), s32[]{:S(2)}) async-start(), calls=%async_computation.7 | async-start | bytes 131072 | tf_op jit(solution)/shard_map/psum | solution.py:17
  615.2 141.6 %all-reduce.53.cloned.1.call-start = ((), (), s32[]{:S(2)}) async-start(), calls=%async_computation.8 | async-start | bytes 131072 | tf_op jit(solution)/shard_map/psum | solution.py:17
  687.3 145.3 %all-reduce.55.cloned.1.call-start = ((), (), s32[]{:S(2)}) async-start(), calls=%async_computation.9 | async-start | bytes 131072 | tf_op jit(solution)/shard_map/psum | solution.py:17
  763.3 146.7 %all-reduce.97.cloned.1.call-start = ((), (), s32[]{:S(2)}) async-start(), calls=%async_computation.30 | async-start | bytes 262144 | tf_op jit(solution)/shard_map/psum | solution.py:17
  839.2 151.5 %all-reduce.57.cloned.1.call-start = ((), (), s32[]{:S(2)}) async-start(), calls=%async_computation.10 | async-start | bytes 131072 | tf_op jit(solution)/shard_map/psum | solution.py:17
  922.2 144.4 %all-reduce.59.cloned.1.call-start = ((), (), s32[]{:S(2)}) async-start(), calls=%async_computation.11 | async-start | bytes 131072 | tf_op jit(solution)/shard_map/psum | solution.py:17
  997.2 145.1 %all-reduce.61.cloned.1.call-start = ((), (), s32[]{:S(2)}) async-start(), calls=%async_computation.12 | async-start | bytes 131072 | tf_op jit(solution)/shard_map/psum | solution.py:17
  1073.1 107.2 %all-reduce.63.cloned.1.call-start = ((), (), s32[]{:S(2)}) async-start(), calls=%async_computation.13 | async-start | bytes 131072 | tf_op jit(solution)/shard_map/psum | solution.py:110
  1148.7 123.4 %all-reduce.65.cloned.1.call-start = ((), (), s32[]{:S(2)}) async-start(), calls=%async_computation.14 | async-start | bytes 131072 | tf_op jit(solution)/shard_map/psum | solution.py:17
  1206.4 141.6 %all-reduce.67.cloned.1.call-start = ((), (), s32[]{:S(2)}) async-start(), calls=%async_computation.15 | async-start | bytes 131072 | tf_op jit(solution)/shard_map/psum | solution.py:17
  1278.5 145.3 %all-reduce.69.cloned.1.call-start = ((), (), s32[]{:S(2)}) async-start(), calls=%async_computation.16 | async-start | bytes 131072 | tf_op jit(solution)/shard_map/psum | solution.py:17
  1354.5 146.6 %all-reduce.95.cloned.1.call-start = ((), (), s32[]{:S(2)}) async-start(), calls=%async_computation.29 | async-start | bytes 262144 | tf_op jit(solution)/shard_map/psum | solution.py:17
  1430.3 151.4 %all-reduce.71.cloned.1.call-start = ((), (), s32[]{:S(2)}) async-start(), calls=%async_computation.17 | async-start | bytes 131072 | tf_op jit(solution)/shard_map/psum | solution.py:17
  1513.1 144.3 %all-reduce.73.cloned.1.call-start = ((), (), s32[]{:S(2)}) async-start(), calls=%async_computation.18 | async-start | bytes 131072 | tf_op jit(solution)/shard_map/psum | solution.py:17
  1588.1 145.1 %all-reduce.75.cloned.1.call-start = ((), (), s32[]{:S(2)}) async-start(), calls=%async_computation.19 | async-start | bytes 131072 | tf_op jit(solution)/shard_map/psum | solution.py:17
  1664.0 107.3 %all-reduce.77.cloned.1.call-start = ((), (), s32[]{:S(2)}) async-start(), calls=%async_computation.20 | async-start | bytes 131072 | tf_op jit(solution)/shard_map/psum | solution.py:110
  1739.6 123.4 %all-reduce.79.cloned.1.call-start = ((), (), s32[]{:S(2)}) async-start(), calls=%async_computation.21 | async-start | bytes 131072 | tf_op jit(solution)/shard_map/psum | solution.py:17
  1797.3 141.6 %all-reduce.81.cloned.1.call-start = ((), (), s32[]{:S(2)}) async-start(), calls=%async_computation.22 | async-start | bytes 131072 | tf_op jit(solution)/shard_map/psum | solution.py:17
  1869.4 145.3 %all-reduce.83.cloned.1.call-start = ((), (), s32[]{:S(2)}) async-start(), calls=%async_computation.23 | async-start | bytes 131072 | tf_op jit(solution)/shard_map/psum | solution.py:17
  1945.4 146.6 %all-reduce.93.cloned.1.call-start = ((), (), s32[]{:S(2)}) async-start(), calls=%async_computation.28 | async-start | bytes 262144 | tf_op jit(solution)/shard_map/psum | solution.py:17
  2021.2 151.4 %all-reduce.85.cloned.1.call-start = ((), (), s32[]{:S(2)}) async-start(), calls=%async_computation.24 | async-start | bytes 131072 | tf_op jit(solution)/shard_map/psum | solution.py:17
  2104.1 144.3 %all-reduce.87.cloned.1.call-start = ((), (), s32[]{:S(2)}) async-start(), calls=%async_computation.25 | async-start | bytes 131072 | tf_op jit(solution)/shard_map/psum | solution.py:17
  2179.1 145.1 %all-reduce.89.cloned.1.call-start = ((), (), s32[]{:S(2)}) async-start(), calls=%async_computation.26 | async-start | bytes 131072 | tf_op jit(solution)/shard_map/psum | solution.py:17
  2255.0 107.5 %all-reduce.91.cloned.1.call-start = ((), (), s32[]{:S(2)}) async-start(), calls=%async_computation.27 | async-start | bytes 131072 | tf_op jit(solution)/shard_map/psum | solution.py:110
  (37 other events, 5737.2 us)
Sparse Core Ops, SparseCore 0:
  18.8 72.1 all-reduce.36
  97.6 69.3 all-reduce.38
  173.5 69.1 all-reduce.40
  249.4 70.6 all-reduce.98
  331.1 68.3 all-reduce.42
  406.1 69.1 all-reduce.44
  482.0 69.0 all-reduce.46
  557.6 31.4 all-reduce.48
  615.4 65.5 all-reduce.50
  687.5 69.3 all-reduce.52
  763.4 69.1 all-reduce.54
  839.3 70.6 all-reduce.96
  922.3 68.3 all-reduce.56
  997.3 69.1 all-reduce.58
  1073.2 69.0 all-reduce.60
  1148.8 31.4 all-reduce.62
  1206.5 65.5 all-reduce.64
  1278.7 69.3 all-reduce.66
  1354.6 69.1 all-reduce.68
  1430.4 70.6 all-reduce.94
  1513.3 68.3 all-reduce.70
  1588.2 69.1 all-reduce.72
  1664.1 69.0 all-reduce.74
  1739.8 31.4 all-reduce.76
  1797.5 65.5 all-reduce.78
  1869.6 69.3 all-reduce.80
  1945.5 69.1 all-reduce.82
  2021.3 70.6 all-reduce.92
  2104.2 68.3 all-reduce.84
  2179.2 69.1 all-reduce.86
  2255.1 69.0 all-reduce.88
  2330.9 31.4 all-reduce.90
where the time goes:
time: 2380 us; the launch traced here: 2370 us
  waiting for transfers between devices  1990 us (84%)
  matrix products  247 us (10%)
  blocking collectives  87.1 us (4%)
  between operations  35.6 us (1%)
    psum x28, waiting for transfers between devices, sum_block(): return lax.psum(stacked, 'people')  1860 us
    psum x4, waiting for transfers between devices, per_device(): residual = start_residual + lax.psum(local_changes, 'snps')  122 us
    dot_general x64, matrix products, contract_last(): lax.dot_general(left, right, (((1,), (1,)), ((), ())), preferred_element_...  93 us
    psum x4, blocking collectives, per_device(): sum_squares = lax.psum(local_squares, 'people')  87.1 us
    dot_general x32, matrix products, per_device(): jnp.dot(state.astype(jnp.bfloat16), block_x, preferred_element_type=jnp.f...  60.1 us
    dot_general x32, matrix products, sample_block(): jnp.dot((summed_row + coupled).astype(jnp.bfloat16), block_basis, preferr...  54.1 us
  transfers between devices with their start and end apart: 32, of which 32 were waited for; matrix products, arithmetic and copies ran while one was open for 2% of the time, Pallas kernels for 0%

commit v1 on v0

v1 whole, which is shorter than its diff:
```python
import functools

import jax
import jax.numpy as jnp
from jax import lax
from jax.experimental import pallas as pl
from jax.experimental.pallas import tpu as pltpu
from jax.sharding import PartitionSpec as P

WINDOW = 4
GROUPS_DEV = 2
VMEM = pltpu.MemorySpace.VMEM
LIMIT = 56 * 1024 * 1024


def dot(left, right):
    return jnp.dot(left, right, preferred_element_type=jnp.float32)


def dot_t(left, right):
    return lax.dot_general(
        left, right, (((1,), (1,)), ((), ())), preferred_element_type=jnp.float32
    )


def permute_kernel(
    people_total, order, x, basis, effects, draws, freq, scale, eig,
    x_out, basis_out, effects_out, draws_out, freq_out, scale_out, eig_out,
):
    x_out[0] = x[...]
    basis_out[...] = basis[...]
    effects_out[0] = effects[...]
    draws_out[:, 0] = draws[...].astype(jnp.float32)
    allele = freq[...]
    freq_out[...] = allele
    scale_out[...] = scale[...] / jnp.sqrt(people_total * 2.0 * allele * (1.0 - allele))
    eig_out[...] = eig[...]


def to_slots(people_total, assignment, genotype, ld_basis, effects, draws, freq, scale, eig):
    blocks, width = ld_basis.shape[0], ld_basis.shape[1]
    people = genotype.shape[0]
    traits = effects.shape[0]
    rounds = draws.shape[0]
    row = lambda s, a: (a[s], 0, 0)
    row_out = lambda s, a: (s, 0, 0)
    return pl.pallas_call(
        functools.partial(permute_kernel, people_total),
        grid_spec=pltpu.PrefetchScalarGridSpec(
            num_scalar_prefetch=1,
            grid=(blocks,),
            in_specs=[
                pl.BlockSpec((people, width), lambda s, a: (0, a[s])),
                pl.BlockSpec((1, width, width), row),
                pl.BlockSpec((traits, width), lambda s, a: (0, a[s])),
                pl.BlockSpec((rounds, traits, width), lambda s, a: (0, 0, a[s])),
                pl.BlockSpec((1, 1, width), row),
                pl.BlockSpec((1, 1, width), row),
                pl.BlockSpec((1, 1, width), row),
            ],
            out_specs=[
                pl.BlockSpec((1, people, width), row_out),
                pl.BlockSpec((1, width, width), row_out),
                pl.BlockSpec((1, traits, width), row_out),
                pl.BlockSpec((rounds, 1, traits, width), lambda s, a: (0, s, 0, 0)),
                pl.BlockSpec((1, 1, width), row_out),
                pl.BlockSpec((1, 1, width), row_out),
                pl.BlockSpec((1, 1, width), row_out),
            ],
        ),
        out_shape=[
            jax.ShapeDtypeStruct((blocks, people, width), genotype.dtype),
            jax.ShapeDtypeStruct((blocks, width, width), ld_basis.dtype),
            jax.ShapeDtypeStruct((blocks, traits, width), jnp.float32),
            jax.ShapeDtypeStruct((rounds, blocks, traits, width), jnp.float32),
            jax.ShapeDtypeStruct((blocks, 1, width), jnp.float32),
            jax.ShapeDtypeStruct((blocks, 1, width), jnp.float32),
            jax.ShapeDtypeStruct((blocks, 1, width), jnp.float32),
        ],
        name="to_slots",
    )(
        assignment, genotype, ld_basis, effects, draws,
        freq.reshape(blocks, 1, width), scale.reshape(blocks, 1, width),
        eig.reshape(blocks, 1, width),
    )


def unpermute_kernel(order, source, target):
    target[...] = source[0]


def from_slots(assignment, effects):
    blocks, traits, width = effects.shape
    return pl.pallas_call(
        unpermute_kernel,
        grid_spec=pltpu.PrefetchScalarGridSpec(
            num_scalar_prefetch=1,
            grid=(blocks,),
            in_specs=[pl.BlockSpec((1, traits, width), lambda s, a: (s, 0, 0))],
            out_specs=pl.BlockSpec((traits, width), lambda s, a: (0, a[s])),
        ),
        out_shape=jax.ShapeDtypeStruct((traits, blocks * width), jnp.float32),
        name="from_slots",
    )(assignment, effects)


def gibbs_kernel(
    people_n, snps_n, people_total,
    x, basis, effects_in, draws, freq, scale, eig, ridge, noise, residual_in,
    effects, residual,
    states, part, gathered, changes, deltas, own_effects,
    part_send, part_recv, change_send, change_recv, delta_send, delta_recv,
):
    me = lax.axis_index("people")
    my_snps = lax.axis_index("snps")
    traits, people = residual_in.shape
    width = scale.shape[-1]
    rounds = draws.shape[0]
    rows = GROUPS_DEV * traits // people_n
    subs = traits // rows
    my_group = me // subs
    my_sub = me % subs

    barrier = pltpu.get_barrier_semaphore()
    for step in range(1, people_n):
        pl.semaphore_signal(
            barrier, inc=1, device_id={"people": lax.rem(me + step, people_n)},
            device_id_type=pl.DeviceIdType.MESH,
        )
    for step in range(1, snps_n):
        pl.semaphore_signal(
            barrier, inc=1, device_id={"snps": lax.rem(my_snps + step, snps_n)},
            device_id_type=pl.DeviceIdType.MESH,
        )

    residual[...] = residual_in[...]
    effects[...] = effects_in[...]
    for group in range(GROUPS_DEV):
        states[group] = residual_in[...]
    mine = pl.ds(my_sub * rows, rows)
    for slot in range(WINDOW):
        own_effects[slot] = effects_in[my_group * WINDOW + slot, mine, :]
    my_ridge = ridge[mine, :]
    my_noise = noise[mine, :]
    pl.semaphore_wait(barrier, people_n - 1 + snps_n - 1)

    def round_body(round_idx, carry):
        squares = jnp.sum(residual[...] * residual[...], axis=1, keepdims=True)
        spread = None
        for slot in range(WINDOW):
            for group in range(GROUPS_DEV):
                block = group * WINDOW + slot
                state = states[group]
                cross = dot(state.astype(jnp.bfloat16), x[block])
                cross = cross - 2.0 * freq[block] * jnp.sum(state, axis=1, keepdims=True)
                for sub in range(subs):
                    part[group * subs + sub, :, :width] = cross[sub * rows:(sub + 1) * rows]
                    if slot == 0:
                        part[group * subs + sub, :, width:] = jnp.broadcast_to(
                            squares[sub * rows:(sub + 1) * rows], (rows, 128)
                        )
            span = width + 128 if slot == 0 else width
            part_copies = []
            for step in range(1, people_n):
                target = lax.rem(me + step, people_n)
                copy = pltpu.make_async_remote_copy(
                    src_ref=part.at[target, :, pl.ds(0, span)],
                    dst_ref=gathered.at[step, :, pl.ds(0, span)],
                    send_sem=part_send.at[step],
                    recv_sem=part_recv.at[step],
                    device_id={"people": target},
                    device_id_type=pl.DeviceIdType.MESH,
                )
                copy.start()
                part_copies.append(copy)

            my_block = my_group * WINDOW + slot
            my_basis = basis[my_block]
            my_eig = eig[my_block]
            my_scale = scale[my_block]
            old = own_effects[slot]
            prior = dot(old.astype(jnp.bfloat16), my_basis)
            coupled = dot_t((prior * my_eig).astype(jnp.bfloat16), my_basis)
            precision = my_eig + my_ridge
            jitter = draws[round_idx, my_block, mine, :] / jnp.sqrt(precision)

            for copy in part_copies:
                copy.wait_recv()
            total = part[me, :, :width]
            for step in range(1, people_n):
                total = total + gathered[step, :, :width]
            if slot == 0:
                total_squares = part[me, :, width:]
                for step in range(1, people_n):
                    total_squares = total_squares + gathered[step, :, width:]
                spread = my_noise * jnp.sqrt(total_squares[:, :1] / people_total + 1e-06)
            rotated = dot((my_scale * total + coupled).astype(jnp.bfloat16), my_basis)
            sampled = rotated / precision + spread * jitter
            fresh = dot_t(sampled.astype(jnp.bfloat16), my_basis)
            own_effects[slot] = fresh
            changes[me] = fresh - old

            change_copies = []
            for step in range(1, people_n):
                target = lax.rem(me + step, people_n)
                copy = pltpu.make_async_remote_copy(
                    src_ref=changes.at[me],
                    dst_ref=changes.at[me],
                    send_sem=change_send.at[step],
                    recv_sem=change_recv.at[step],
                    device_id={"people": target},
                    device_id_type=pl.DeviceIdType.MESH,
                )
                copy.start()
                change_copies.append(copy)
            for copy in part_copies:
                copy.wait_send()
            for copy in change_copies:
                copy.wait()
            for group in range(GROUPS_DEV):
                block = group * WINDOW + slot
                pieces = [changes[group * subs + sub] for sub in range(subs)]
                change = pieces[0] if subs == 1 else jnp.concatenate(pieces, axis=0)
                weighted = change * scale[block]
                shift = 2.0 * jnp.sum(weighted * freq[block], axis=1, keepdims=True)
                states[group] = (
                    states[group] - dot_t(weighted.astype(jnp.bfloat16), x[block]) + shift
                )
                effects[block] = effects[block] + change

        bank = lax.rem(round_idx, 2)
        delta = states[0] - residual[...]
        for group in range(1, GROUPS_DEV):
            delta = delta + (states[group] - residual[...])
        deltas[bank, my_snps] = delta
        delta_copies = []
        for step in range(1, snps_n):
            target = lax.rem(my_snps + step, snps_n)
            copy = pltpu.make_async_remote_copy(
                src_ref=deltas.at[bank, my_snps],
                dst_ref=deltas.at[bank, my_snps],
                send_sem=delta_send.at[bank, step],
                recv_sem=delta_recv.at[bank, step],
                device_id={"snps": target},
                device_id_type=pl.DeviceIdType.MESH,
            )
            copy.start()
            delta_copies.append(copy)
        for copy in delta_copies:
            copy.wait()
        total = deltas[bank, 0]
        for index in range(1, snps_n):
            total = total + deltas[bank, index]
        fresh_residual = residual[...] + total
        residual[...] = fresh_residual
        for group in range(GROUPS_DEV):
            states[group] = fresh_residual
        return carry

    lax.fori_loop(0, rounds, round_body, 0)


def per_device(people_n, snps_n, genotype, residual_init, effects_init, allele_freq, snp_scale,
               ld_basis, ld_eig, ridge, noise_scale, normal_draws, assignment):
    traits, people = residual_init.shape
    width = ld_basis.shape[1]
    people_total = people * people_n
    x, basis, effects_in, draws, freq, scale, eig = to_slots(
        people_total, assignment, genotype, ld_basis, effects_init, normal_draws,
        allele_freq, snp_scale, ld_eig,
    )
    rows = GROUPS_DEV * traits // people_n
    effects, residual = pl.pallas_call(
        functools.partial(gibbs_kernel, people_n, snps_n, people_total),
        out_shape=[
            jax.ShapeDtypeStruct(effects_in.shape, jnp.float32),
            jax.ShapeDtypeStruct((traits, people), jnp.float32),
        ],
        in_specs=[pl.BlockSpec(memory_space=VMEM)] * 10,
        out_specs=[pl.BlockSpec(memory_space=VMEM)] * 2,
        scratch_shapes=[
            pltpu.VMEM((GROUPS_DEV, traits, people), jnp.float32),
            pltpu.VMEM((people_n, rows, width + 128), jnp.float32),
            pltpu.VMEM((people_n, rows, width + 128), jnp.float32),
            pltpu.VMEM((people_n, rows, width), jnp.float32),
            pltpu.VMEM((2, snps_n, traits, people), jnp.float32),
            pltpu.VMEM((WINDOW, rows, width), jnp.float32),
            pltpu.SemaphoreType.DMA((people_n,)),
            pltpu.SemaphoreType.DMA((people_n,)),
            pltpu.SemaphoreType.DMA((people_n,)),
            pltpu.SemaphoreType.DMA((people_n,)),
            pltpu.SemaphoreType.DMA((2, snps_n)),
            pltpu.SemaphoreType.DMA((2, snps_n)),
        ],
        compiler_params=pltpu.CompilerParams(
            collective_id=0, has_side_effects=True, vmem_limit_bytes=LIMIT
        ),
        name="gibbs",
    )(
        x, basis, effects_in, draws, freq, scale, eig,
        ridge.reshape(traits, 1), noise_scale.reshape(traits, 1), residual_init,
    )
    return from_slots(assignment, effects), residual


def solution(mesh):
    return jax.shard_map(
        functools.partial(per_device, mesh.shape["people"], mesh.shape["snps"]),
        mesh=mesh,
        in_specs=(
            P("people", "snps"),
            P(None, "people"),
            P(None, "snps"),
            P("snps"),
            P("snps"),
            P("snps", None, None),
            P("snps"),
            P(),
            P(),
            P(None, None, "snps"),
            P("snps"),
        ),
        out_specs=(P(None, "snps"), P(None, "people")),
        check_vma=False,
    )
```

time: 2380 us -> 221 us (0.09)
  waiting for transfers between devices: 1990 us -> 0 us
  matrix products: 247 us -> 0 us
  Pallas kernels: 0 us -> 215 us
  blocking collectives: 87.1 us -> 0 us
  between operations: 35.6 us -> 0.64 us
    psum x32 -> x0, waiting for transfers between devices: 1990 us -> none  [the longest x28 1860 us: sum_block(): return lax.psum(stacked, 'people')]
    dot_general x160 -> x0, matrix products: 247 us -> none  [the longest x64 93 us: contract_last(): lax.dot_general(left, right, (((1,), (1,)), ((), ())), preferred_element_...]
    pallas_call x0 -> x3, Pallas kernels: none -> 215 us  [the longest x1 199 us: per_device(): pl.pallas_call(functools.partial(gibbs_kernel, people_n, snps_n, people_t...]
    psum x4 -> x0, blocking collectives: 87.1 us -> none  [per_device(): sum_squares = lax.psum(local_squares, 'people')]
  transfers between devices with their start and end apart: 32 -> 0, of which waited for: 32 -> 0; matrix products, arithmetic and copies ran while one was open for 2% -> 0% of each run, Pallas kernels for 0% -> 0%
where the time goes in v1:
time: 221 us; the launch traced here: 220 us
  Pallas kernels  215 us (97%)
  local copies, waits for them, and re-layouts  4.14 us (2%)
    pallas_call x1, Pallas kernels, per_device(): pl.pallas_call(functools.partial(gibbs_kernel, people_n, snps_n, people_t...  199 us
    pallas_call x1, Pallas kernels, to_slots(): pl.pallas_call(functools.partial(permute_kernel, people_total), grid_spec...  10.8 us
    pallas_call x1, Pallas kernels, from_slots(): pl.pallas_call(unpermute_kernel, grid_spec=pltpu.PrefetchScalarGridSpec(n...  5.41 us

profile of v1, /device:TPU:0, one launch (start us, length us, event | category | flops | bytes accessed | tf_op | source)
XLA Modules:
  0.0 220.0 jit_solution(69021154012937707)
XLA Ops:
  0.6 1.3 copy.13.ridge
  2.0 1.3 copy.14.noise
  3.3 10.8 %to_slots.1 = (bf16[8,512,512]{2,1,0:T(8,128)(2,1)}, bf16[8,512,512]{2,1,0:T(8,128)(2,1)}, f32[8,32,512]{2,1,0:T(8,128)}, f32[4,8,32,512]{3,2,1,0:T(8,128)}, f32...) custom-call(s32[8]{0:T(128)} %order.3, bf16[512,4096]{1,0:T(8,128)(2,1)} %x.1, ...), custom_call_target="tpu_custom_call" | custom-call | tf_op jit(solution)/shard_map/to_slots/pallas_call | solution.py:47
  14.1 199.1 %gibbs.1 = (f32[8,32,512]{2,1,0:T(8,128)}, f32[32,512]{1,0:T(8,128)}) custom-call(bf16[8,512,512]{2,1,0:T(8,128)(2,1)} %get-tuple-element.11.x, bf16[8,512,512]{2,1,0:T(8,128)(2,1)} %get-tuple-element.12.basis, f32[8,32,512]{2,1,0:T(8,128)} %get-tuple-element.13.effects_in, f32[4,8,32,512]{3,2,1,0:T(8,128)} %get-tuple-element.14.draws, ...), custom_call_target="tpu_custom_call" | custom-call | tf_op jit(solution)/shard_map/gibbs/pallas_call | solution.py:273
  213.2 5.4 %from_slots.1 = f32[32,4096]{1,0:T(8,128)} custom-call(s32[8]{0:T(128)} %order.3, f32[8,32,512]{2,1,0:T(8,128)} %get-tuple-element.18.source), custom_call_target="tpu_custom_call" | custom-call | tf_op jit(solution)/shard_map/from_slots/pallas_call | solution.py:94
  218.6 1.5 copy.16

commit v2 on v0

v2 whole, which is shorter than its diff:
```python
import functools

import jax
import jax.numpy as jnp
from jax import lax
from jax.experimental import pallas as pl
from jax.experimental.pallas import tpu as pltpu
from jax.sharding import PartitionSpec as P

WINDOW = 4
GROUPS_DEV = 2
LIMIT = 56 * 1024 * 1024
MESH = pl.DeviceIdType.MESH


def dot(left, right):
    return jnp.dot(left, right, preferred_element_type=jnp.float32)


def dot_t(left, right):
    return lax.dot_general(
        left, right, (((1,), (1,)), ((), ())), preferred_element_type=jnp.float32
    )


def as_column(row):
    size = row.shape[1]
    across = lax.broadcasted_iota(jnp.int32, (size, size), 1)
    down = lax.broadcasted_iota(jnp.int32, (size, size), 0)
    spread_out = jnp.broadcast_to(row, (size, size))
    return jnp.sum(jnp.where(across == down, spread_out, 0.0), axis=1, keepdims=True)


def gibbs_kernel(
    people_n, snps_n, people_total,
    genotype_hbm, basis_hbm, draws_hbm, effects_hbm, freq, snp_scale, eig, ridge, noise,
    residual_in, assignment, inverse,
    effects, residual,
    genotype, basis, draws, effects_in, scale, slot_effects, states, part, gathered, changes, deltas,
    own_effects, own_draws, own_traits, own_spread,
    load_sem, part_send, part_recv, change_send, change_recv, delta_send, delta_recv,
):
    me = lax.axis_index("people")
    my_snps = lax.axis_index("snps")
    traits, people = residual_in.shape
    blocks, width = basis.shape[0], basis.shape[1]
    rounds = draws.shape[1]
    owners, rows = part.shape[0], part.shape[1]
    first = (people_n - owners) // 2
    subs = owners // GROUPS_DEV
    owner_here = (me >= first) & (me < first + owners)
    mine = me - first
    my_group = mine // subs
    my_rows = pl.ds((mine % subs) * rows, rows)

    loads = [pltpu.make_async_copy(basis_hbm, basis, load_sem.at[3 * blocks])]
    for block in range(blocks):
        cols = pl.ds(block * width, width)
        loads += [
            pltpu.make_async_copy(effects_hbm.at[:, cols], effects_in.at[block], load_sem.at[block]),
            pltpu.make_async_copy(
                genotype_hbm.at[:, cols], genotype.at[block], load_sem.at[blocks + block]
            ),
            pltpu.make_async_copy(
                draws_hbm.at[:, :, cols], draws.at[block], load_sem.at[2 * blocks + block]
            ),
        ]
    for load in loads:
        load.start()

    barrier = pltpu.get_barrier_semaphore()
    for step in range(1, people_n):
        pl.semaphore_signal(
            barrier, inc=1, device_id={"people": lax.rem(me + step, people_n)},
            device_id_type=MESH,
        )
    for step in range(1, snps_n):
        pl.semaphore_signal(
            barrier, inc=1, device_id={"snps": lax.rem(my_snps + step, snps_n)},
            device_id_type=MESH,
        )

    allele = freq[...]
    scale[...] = snp_scale[...] / jnp.sqrt(people_total * 2.0 * allele * (1.0 - allele))
    residual[...] = residual_in[...]
    for group in range(GROUPS_DEV):
        states[group] = residual_in[...]
    own_traits[0] = jnp.broadcast_to(as_column(ridge[...]), (traits, 128))
    own_traits[1] = jnp.broadcast_to(as_column(noise[...]), (traits, 128))

    def part_copy(owner, step, span):
        return pltpu.make_async_remote_copy(
            src_ref=part.at[owner - first, :, pl.ds(0, span)],
            dst_ref=gathered.at[step, :, pl.ds(0, span)],
            send_sem=part_send.at[owner - first],
            recv_sem=part_recv.at[step],
            device_id={"people": owner},
            device_id_type=MESH,
        )

    def change_copy(owner, target, bank):
        return pltpu.make_async_remote_copy(
            src_ref=changes.at[bank, owner],
            dst_ref=changes.at[bank, owner],
            send_sem=change_send.at[bank, target],
            recv_sem=change_recv.at[bank, owner],
            device_id={"people": target},
            device_id_type=MESH,
        )

    def far_first(index, count):
        return jnp.where(me < people_n // 2, count - 1 - index, index)

    def span_of(slot):
        return width + 128 if slot == 0 else width

    def send_parts(slot, group, squares):
        block = group * WINDOW + slot
        held = assignment[block]
        state = states[group]
        cross = dot(state.astype(jnp.bfloat16), genotype[held])
        cross = cross - 2.0 * freq[held] * jnp.sum(state, axis=1, keepdims=True)
        for sub in range(subs):
            owner = group * subs + sub
            part[owner, :, :width] = cross[sub * rows:(sub + 1) * rows]
            if slot == 0:
                part[owner, :, width:] = jnp.broadcast_to(
                    squares[sub * rows:(sub + 1) * rows], (rows, 128)
                )
        for index in range(subs):
            owner = first + group * subs + far_first(index, subs)

            @pl.when(owner != me)
            def _():
                part_copy(owner, lax.rem(me - owner + people_n, people_n), span_of(slot)).start()

    def sample(round_idx, slot):
        bank = slot % 2
        my_block = my_group * WINDOW + slot
        held = assignment[my_block]
        my_basis = basis[held]
        my_eig = eig[held]
        my_scale = scale[held]
        own_draws[...] = draws[held, round_idx].astype(jnp.float32)
        old = own_effects[slot]
        prior = dot(old.astype(jnp.bfloat16), my_basis)
        coupled = dot_t((prior * my_eig).astype(jnp.bfloat16), my_basis)
        precision = my_eig + own_traits[0, my_rows, :][:, :1]
        jitter = own_draws[my_rows, :] / jnp.sqrt(precision)
        for step in range(1, people_n):
            part_copy(me, step, span_of(slot)).wait_recv()
        total = part[mine, :, :width]
        for step in range(1, people_n):
            total = total + gathered[step, :, :width]
        if slot == 0:
            squares = part[mine, :, width:]
            for step in range(1, people_n):
                squares = squares + gathered[step, :, width:]
            own_spread[...] = own_traits[1, my_rows, :] * jnp.sqrt(squares / people_total + 1e-06)
        spread = own_spread[...][:, :1]
        rotated = dot((my_scale * total + coupled).astype(jnp.bfloat16), my_basis)
        sampled = rotated / precision + spread * jitter
        fresh = dot_t(sampled.astype(jnp.bfloat16), my_basis)
        own_effects[slot] = fresh
        changes[bank, mine] = fresh - old
        for index in range(people_n):
            target = far_first(index, people_n)

            @pl.when(target != me)
            def _():
                change_copy(mine, target, bank).start()

    def change_of(slot, group):
        bank = slot % 2
        pieces = [changes[bank, group * subs + sub] for sub in range(subs)]
        return pieces[0] if subs == 1 else jnp.concatenate(pieces, axis=0)

    def take_changes(slot, group):
        bank = slot % 2
        block = group * WINDOW + slot
        for sub in range(subs):
            owner = group * subs + sub

            @pl.when(me != first + owner)
            def _():
                change_copy(owner, 0, bank).wait_recv()
                part_copy(first + owner, 1, span_of(slot)).wait_send()

        held = assignment[block]
        weighted = change_of(slot, group) * scale[held]
        shift = 2.0 * jnp.sum(weighted * freq[held], axis=1, keepdims=True)
        states[group] = (
            states[group] - dot_t(weighted.astype(jnp.bfloat16), genotype[held]) + shift
        )

    def settle(slot):
        for group in range(GROUPS_DEV):
            block = group * WINDOW + slot
            slot_effects[block] = slot_effects[block] + change_of(slot, group)

        @pl.when(owner_here)
        def _():
            for target in range(people_n):
                @pl.when(target != me)
                def _():
                    change_copy(mine, target, slot % 2).wait_send()

    for load in loads:
        load.wait()
    for block in range(blocks):
        slot_effects[block] = effects_in[assignment[block]]

    @pl.when(owner_here)
    def _():
        for slot in range(WINDOW):
            own_effects[slot] = slot_effects[my_group * WINDOW + slot, my_rows, :]

    pl.semaphore_wait(barrier, people_n - 1 + snps_n - 1)

    def round_body(round_idx, carry):
        squares = jnp.sum(residual[...] * residual[...], axis=1, keepdims=True)
        for slot in range(WINDOW):
            for group in range(GROUPS_DEV):
                if slot > 0:
                    take_changes(slot - 1, group)
                send_parts(slot, group, squares)
            if slot > 0:
                settle(slot - 1)

            @pl.when(owner_here)
            def _():
                sample(round_idx, slot)

        for group in range(GROUPS_DEV):
            take_changes(WINDOW - 1, group)
        bank = lax.rem(round_idx, 2)
        delta = states[0] - residual[...]
        for group in range(1, GROUPS_DEV):
            delta = delta + (states[group] - residual[...])
        deltas[bank, my_snps] = delta
        delta_copies = []
        for step in range(1, snps_n):
            copy = pltpu.make_async_remote_copy(
                src_ref=deltas.at[bank, my_snps],
                dst_ref=deltas.at[bank, my_snps],
                send_sem=delta_send.at[bank, step],
                recv_sem=delta_recv.at[bank, step],
                device_id={"snps": lax.rem(my_snps + step, snps_n)},
                device_id_type=MESH,
            )
            copy.start()
            delta_copies.append(copy)
        settle(WINDOW - 1)
        for copy in delta_copies:
            copy.wait()
        total = deltas[bank, 0]
        for index in range(1, snps_n):
            total = total + deltas[bank, index]
        fresh_residual = residual[...] + total
        residual[...] = fresh_residual
        for group in range(GROUPS_DEV):
            states[group] = fresh_residual
        return carry

    lax.fori_loop(0, rounds, round_body, 0)

    for target in range(blocks):
        effects[:, target * width:(target + 1) * width] = slot_effects[inverse[target]]


def owner_count(people_n, traits):
    return max(min(people_n // 2, GROUPS_DEV * traits // 8), GROUPS_DEV)


def per_device(people_n, snps_n, genotype, residual_init, effects_init, allele_freq, snp_scale,
               ld_basis, ld_eig, ridge, noise_scale, normal_draws, assignment):
    traits, people = residual_init.shape
    blocks, width = ld_basis.shape[0], ld_basis.shape[1]
    owners = owner_count(people_n, traits)
    rows = GROUPS_DEV * traits // owners
    slots = jnp.arange(blocks, dtype=jnp.int32)
    inverse = jnp.sum(
        jnp.where(assignment[None, :] == slots[:, None], slots[None, :], 0), axis=1, dtype=jnp.int32
    )
    by_block = lambda values: values.reshape(blocks, 1, width)
    row = lambda values: values.reshape(1, values.shape[0])
    vmem = pl.BlockSpec(memory_space=pltpu.MemorySpace.VMEM)
    smem = pl.BlockSpec(memory_space=pltpu.MemorySpace.SMEM)
    far = pl.BlockSpec(memory_space=pl.ANY)
    return pl.pallas_call(
        functools.partial(gibbs_kernel, people_n, snps_n, people * people_n),
        out_shape=[
            jax.ShapeDtypeStruct(effects_init.shape, jnp.float32),
            jax.ShapeDtypeStruct((traits, people), jnp.float32),
        ],
        in_specs=[far] * 4 + [vmem] * 6 + [smem] * 2,
        out_specs=[vmem] * 2,
        scratch_shapes=[
            pltpu.VMEM((blocks, people, width), genotype.dtype),
            pltpu.VMEM(ld_basis.shape, ld_basis.dtype),
            pltpu.VMEM((blocks,) + normal_draws.shape[:2] + (width,), normal_draws.dtype),
            pltpu.VMEM((blocks, traits, width), jnp.float32),
            pltpu.VMEM((blocks, 1, width), jnp.float32),
            pltpu.VMEM((blocks, traits, width), jnp.float32),
            pltpu.VMEM((GROUPS_DEV, traits, people), jnp.float32),
            pltpu.VMEM((owners, rows, width + 128), jnp.float32),
            pltpu.VMEM((people_n, rows, width + 128), jnp.float32),
            pltpu.VMEM((2, owners, rows, width), jnp.float32),
            pltpu.VMEM((2, snps_n, traits, people), jnp.float32),
            pltpu.VMEM((WINDOW, rows, width), jnp.float32),
            pltpu.VMEM((traits, width), jnp.float32),
            pltpu.VMEM((2, traits, 128), jnp.float32),
            pltpu.VMEM((rows, 128), jnp.float32),
            pltpu.SemaphoreType.DMA((3 * blocks + 1,)),
            pltpu.SemaphoreType.DMA((owners,)),
            pltpu.SemaphoreType.DMA((people_n,)),
            pltpu.SemaphoreType.DMA((2, people_n)),
            pltpu.SemaphoreType.DMA((2, owners)),
            pltpu.SemaphoreType.DMA((2, snps_n)),
            pltpu.SemaphoreType.DMA((2, snps_n)),
        ],
        compiler_params=pltpu.CompilerParams(
            collective_id=0, has_side_effects=True, vmem_limit_bytes=LIMIT
        ),
        name="gibbs",
    )(
        genotype, ld_basis, normal_draws, effects_init, by_block(allele_freq),
        by_block(snp_scale), by_block(ld_eig), row(ridge), row(noise_scale), residual_init,
        assignment, inverse,
    )


def solution(mesh):
    return jax.shard_map(
        functools.partial(per_device, mesh.shape["people"], mesh.shape["snps"]),
        mesh=mesh,
        in_specs=(
            P("people", "snps"),
            P(None, "people"),
            P(None, "snps"),
            P("snps"),
            P("snps"),
            P("snps", None, None),
            P("snps"),
            P(),
            P(),
            P(None, None, "snps"),
            P("snps"),
        ),
        out_specs=(P(None, "snps"), P(None, "people")),
        check_vma=False,
    )
```

time: 2380 us -> 200 us (0.08)
  waiting for transfers between devices: 1990 us -> 0 us
  matrix products: 247 us -> 0 us
  Pallas kernels: 0 us -> 194 us
  blocking collectives: 87.1 us -> 0 us
  between operations: 35.6 us -> 0.64 us
    psum x32 -> x0, waiting for transfers between devices: 1990 us -> none  [the longest x28 1860 us: sum_block(): return lax.psum(stacked, 'people')]
    dot_general x160 -> x0, matrix products: 247 us -> none  [the longest x64 93 us: contract_last(): lax.dot_general(left, right, (((1,), (1,)), ((), ())), preferred_element_...]
    pallas_call x0 -> x1, Pallas kernels: none -> 194 us  [per_device(): pl.pallas_call(functools.partial(gibbs_kernel, people_n, snps_n, people *...]
    psum x4 -> x0, blocking collectives: 87.1 us -> none  [per_device(): sum_squares = lax.psum(local_squares, 'people')]
  transfers between devices with their start and end apart: 32 -> 0, of which waited for: 32 -> 0; matrix products, arithmetic and copies ran while one was open for 2% -> 0% of each run, Pallas kernels for 0% -> 0%
where the time goes in v2:
time: 200 us; the launch traced here: 199 us
  Pallas kernels  194 us (97%)
  local copies, waits for them, and re-layouts  3.34 us (2%)
    pallas_call x1, Pallas kernels, per_device(): pl.pallas_call(functools.partial(gibbs_kernel, people_n, snps_n, people *...  194 us

profile of v2, /device:TPU:0, one launch (start us, length us, event | category | flops | bytes accessed | tf_op | source)
XLA Modules:
  0.0 199.1 jit_solution(7595070049270369087)
XLA Ops:
  0.6 1.3 select_reduce_fusion.inverse
  1.9 193.9 %gibbs.1 = (f32[32,4096]{1,0:T(8,128)}, f32[32,512]{1,0:T(8,128)}) custom-call(bf16[512,4096]{1,0:T(8,128)(2,1)} %genotype_hbm.1, bf16[8,512,512]{2,1,0:T(8,128)(2,1)} %basis_hbm.1, bf16[4,32,4096]{2,1,0:T(8,128)(2,1)} %draws_hbm.1, f32[32,4096]{1,0:T(8,128)} %effects_hbm.1, f32[8,1,512]{2,1,0:T(1,128)} %bitcast.5, f32[8,1,512]{2,1,0:T(1,128)} %bitcast.6, ...), custom_call_target="tpu_custom_call" | custom-call | tf_op jit(solution)/shard_map/gibbs/pallas_call | solution.py:290
  195.8 1.9 copy.15
  197.7 1.5 copy.16

commit v3 on v2

--- a/solution.py
+++ b/solution.py
@@ -37,7 +37,7 @@
     residual_in, assignment, inverse,
     effects, residual,
     genotype, basis, draws, effects_in, scale, slot_effects, states, part, gathered, changes, deltas,
-    own_effects, own_draws, own_traits, own_spread,
+    own_effects, own_prior, own_draws, own_traits, own_spread,
     load_sem, part_send, part_recv, change_send, change_recv, delta_send, delta_recv,
 ):
     me = lax.axis_index("people")
@@ -134,19 +134,23 @@
             def _():
                 part_copy(owner, lax.rem(me - owner + people_n, people_n), span_of(slot)).start()
 
-    def sample(round_idx, slot):
-        bank = slot % 2
-        my_block = my_group * WINDOW + slot
-        held = assignment[my_block]
+    def prepare(round_idx, slot):
+        held = assignment[my_group * WINDOW + slot]
         my_basis = basis[held]
         my_eig = eig[held]
+        own_draws[...] = draws[held, round_idx].astype(jnp.float32)
+        prior = dot(own_effects[slot].astype(jnp.bfloat16), my_basis)
+        own_prior[0] = dot_t((prior * my_eig).astype(jnp.bfloat16), my_basis)
+        precision = my_eig + own_traits[0, my_rows, :][:, :1]
+        own_prior[1] = precision
+        own_prior[2] = own_draws[my_rows, :] / jnp.sqrt(precision)
+
+    def sample(slot):
+        bank = slot % 2
+        held = assignment[my_group * WINDOW + slot]
+        my_basis = basis[held]
         my_scale = scale[held]
-        own_draws[...] = draws[held, round_idx].astype(jnp.float32)
         old = own_effects[slot]
-        prior = dot(old.astype(jnp.bfloat16), my_basis)
-        coupled = dot_t((prior * my_eig).astype(jnp.bfloat16), my_basis)
-        precision = my_eig + own_traits[0, my_rows, :][:, :1]
-        jitter = own_draws[my_rows, :] / jnp.sqrt(precision)
         for step in range(1, people_n):
             part_copy(me, step, span_of(slot)).wait_recv()
         total = part[mine, :, :width]
@@ -158,8 +162,8 @@
                 squares = squares + gathered[step, :, width:]
             own_spread[...] = own_traits[1, my_rows, :] * jnp.sqrt(squares / people_total + 1e-06)
         spread = own_spread[...][:, :1]
-        rotated = dot((my_scale * total + coupled).astype(jnp.bfloat16), my_basis)
-        sampled = rotated / precision + spread * jitter
+        rotated = dot((my_scale * total + own_prior[0]).astype(jnp.bfloat16), my_basis)
+        sampled = rotated / own_prior[1] + spread * own_prior[2]
         fresh = dot_t(sampled.astype(jnp.bfloat16), my_basis)
         own_effects[slot] = fresh
         changes[bank, mine] = fresh - old
@@ -214,6 +218,7 @@
     def _():
         for slot in range(WINDOW):
             own_effects[slot] = slot_effects[my_group * WINDOW + slot, my_rows, :]
+        prepare(0, 0)
 
     pl.semaphore_wait(barrier, people_n - 1 + snps_n - 1)
 
@@ -224,12 +229,15 @@
                 if slot > 0:
                     take_changes(slot - 1, group)
                 send_parts(slot, group, squares)
+
+            @pl.when(owner_here)
+            def _():
+                sample(slot)
+                if slot < WINDOW - 1:
+                    prepare(round_idx, slot + 1)
+
             if slot > 0:
                 settle(slot - 1)
-
-            @pl.when(owner_here)
-            def _():
-                sample(round_idx, slot)
 
         for group in range(GROUPS_DEV):
             take_changes(WINDOW - 1, group)
@@ -251,6 +259,11 @@
             copy.start()
             delta_copies.append(copy)
         settle(WINDOW - 1)
+
+        @pl.when(owner_here)
+        def _():
+            prepare(lax.rem(round_idx + 1, rounds), 0)
+
         for copy in delta_copies:
             copy.wait()
         total = deltas[bank, 0]
@@ -308,6 +321,7 @@
             pltpu.VMEM((2, owners, rows, width), jnp.float32),
             pltpu.VMEM((2, snps_n, traits, people), jnp.float32),
             pltpu.VMEM((WINDOW, rows, width), jnp.float32),
+            pltpu.VMEM((3, rows, width), jnp.float32),
             pltpu.VMEM((traits, width), jnp.float32),
             pltpu.VMEM((2, traits, 128), jnp.float32),
             pltpu.VMEM((rows, 128), jnp.float32),

time: 200 us -> 200 us (level)
  no operation moved by 1% of the time
where the time goes in v3:
time: 200 us
  Pallas kernels  194 us (97%)
  local copies, waits for them, and re-layouts  3.34 us (2%)
    pallas_call x1, Pallas kernels, per_device(): pl.pallas_call(functools.partial(gibbs_kernel, people_n, snps_n, people *...  194 us

profile of v3, /device:TPU:0, one launch (start us, length us, event | category | flops | bytes accessed | tf_op | source)
XLA Modules:
  0.0 199.6 jit_solution(11305059936031183159)
XLA Ops:
  0.6 1.3 select_reduce_fusion.inverse
  1.9 194.4 %gibbs.1 = (f32[32,4096]{1,0:T(8,128)}, f32[32,512]{1,0:T(8,128)}) custom-call(bf16[512,4096]{1,0:T(8,128)(2,1)} %genotype_hbm.1, bf16[8,512,512]{2,1,0:T(8,128)(2,1)} %basis_hbm.1, bf16[4,32,4096]{2,1,0:T(8,128)(2,1)} %draws_hbm.1, f32[32,4096]{1,0:T(8,128)} %effects_hbm.1, f32[8,1,512]{2,1,0:T(1,128)} %bitcast.5, f32[8,1,512]{2,1,0:T(1,128)} %bitcast.6, ...), custom_call_target="tpu_custom_call" | custom-call | tf_op jit(solution)/shard_map/gibbs/pallas_call | solution.py:303
  196.3 1.9 copy.15
  198.2 1.5 copy.16
